TPU v7x, 256 devices: a whole 4x4x8 slice. The times are simulated.
256 devices in a mesh: tm: 8 (over x_hi, y), azim: 32 (over z, x_lo, core).
Axes of the slice: x: 4 (x_hi: 2, x_lo: 2; x = x_hi * 2 + x_lo), y: 4, z: 8, core: 2. Of those that a mesh axis runs over, the one named last changes fastest.
Arguments:
- rotor_coeffs: float32 [64, 2, 32, 16384], P('tm', None, 'azim'), may hold values from -1.5 to 1.5
- mortar_weights: float32 [64, 2, 32, 16384], P('tm', None, 'azim'), may hold values from 0.2 to 1
- block_shifts: int32 [64], P('tm'), may hold values from 0 to 31
- stencil_offsets: int32 [64, 2], P('tm'), may hold values from -1 to 1
- reluctivity: float32 [32, 16384], P('azim'), may hold values from 0.5 to 2
- source: float32 [64, 2, 32, 16384], P('tm', None, 'azim'), may hold values from -3 to 3
Outputs:
- residual: float32 [64, 2, 32, 16384], P('tm', None, 'azim')
All inputs are finite; a program needn't handle non-finite values.
Results may differ from a plain program's by a relative error of at most 0.0001.
Values sent between devices are 32-bit elements; how exact they have to be, the bound alone decides.
A program may use at most 128 MiB of HBM per device.

v0:
```python
import itertools
import jax
import jax.numpy as jnp
import numpy as np
from jax import lax
from jax.sharding import PartitionSpec as P

KC = 64
NT = 64
LANES = 128


def shifted(value, axis, steps):
    count = lax.axis_size(axis)
    pairs = [(source, (source + steps) % count) for source in range(count)]
    return lax.ppermute(value, axis, pairs)


def harmonic_basis(sample_rows, coefficient_count):
    column = jnp.arange(coefficient_count, dtype=jnp.int32)
    harmonic_order = 2 * (column // 2) + 1
    phase_index = harmonic_order[None, :] * (2 * sample_rows[:, None] + 1) % (4 * NT)
    phase_angle = phase_index.astype(jnp.float32) * (jnp.pi / (2 * NT))
    return jnp.where(column[None, :] % 2 == 0, jnp.cos(phase_angle), jnp.sin(phase_angle))


def per_sample(flags, value):
    return flags.reshape((-1,) + (1,) * (value.ndim - 1))


def digit_table(stages, count):
    found = {}
    for bits in itertools.product((0, 1), repeat=len(stages)):
        found.setdefault(sum((b * s for b, s in zip(bits, stages))) % count, bits)
    return np.array([found[d] for d in range(count)], np.int32)


def barrel(value, amounts, stages, axis):
    count = lax.axis_size(axis)
    picks = jnp.take(jnp.asarray(digit_table(stages, count)), amounts % count, axis=0)
    for level, steps in enumerate(stages):
        moved = shifted(value, axis, steps)
        value = jnp.where(per_sample(picks[:, level] == 1, value), moved, value)
    return value


def body(rotor_coeffs, mortar_weights, block_shifts, stencil_offsets, reluctivity, source):
    local_c, comp, _, nodes = rotor_coeffs.shape
    local_j, sten = mortar_weights.shape[:2]
    rows = nodes // LANES
    parts = lax.axis_size("tm")
    chunk = rows // parts
    coeffs = lax.all_to_all(
        rotor_coeffs.reshape(local_c, comp, rows, LANES),
        "tm",
        split_axis=2,
        concat_axis=0,
        tiled=True,
    )
    weights = lax.all_to_all(
        mortar_weights.reshape(local_j, sten, rows, LANES),
        "tm",
        split_axis=2,
        concat_axis=0,
        tiled=True,
    )
    small = jnp.concatenate([block_shifts[:, None], stencil_offsets], axis=1).astype(jnp.float32)
    small = lax.all_gather(small, "tm", tiled=True).astype(jnp.int32)
    shifts, offsets = (small[:, 0], small[:, 1:])
    gain = lax.dynamic_slice_in_dim(
        reluctivity.reshape(rows, LANES), lax.axis_index("tm") * chunk, chunk, axis=0
    )
    table = harmonic_basis(jnp.arange(NT, dtype=jnp.int32), KC)
    samples = jnp.einsum("jc,capk->japk", table, coeffs, precision=lax.Precision.HIGHEST)
    orders = ((1, 2, 4, -8, 16), (16, 8, -4, 2, 1))
    fields = []
    for component in range(comp):
        turned = barrel(samples[:, component], shifts, orders[component % 2], "azim")
        from_left = shifted(turned, "azim", 1)
        from_right = shifted(turned, "azim", -1)
        field = jnp.zeros_like(turned)
        for stencil_entry in range(sten):
            offset = offsets[:, stencil_entry]
            neighbour = jnp.where(
                per_sample(offset == 0, turned),
                turned,
                jnp.where(per_sample(offset > 0, turned), from_right, from_left),
            )
            field = field + weights[:, stencil_entry] * neighbour
        fields.append(field)
    airgap_field = jnp.stack(fields, axis=1)
    square = jnp.sum(airgap_field * airgap_field, axis=1, keepdims=True)
    field_flux = gain[None, None] * (1.0 + square / (1.0 + square)) * airgap_field
    summed = jnp.einsum(
        "jc,japk->capk", table * (2.0 / NT), field_flux, precision=lax.Precision.HIGHEST
    )
    residual = lax.all_to_all(summed, "tm", split_axis=0, concat_axis=2, tiled=True)
    return residual.reshape(source.shape) - source


def solution(mesh):
    in_specs = (
        P("tm", None, "azim", None),
        P("tm", None, "azim", None),
        P("tm"),
        P("tm", None),
        P("azim", None),
        P("tm", None, "azim", None),
    )
    out_specs = P("tm", None, "azim", None)
    return jax.shard_map(body, mesh=mesh, in_specs=in_specs, out_specs=out_specs, check_vma=False)
```

profile of v0, /device:TPU:1, one launch (start us, length us, event | category | flops | bytes accessed | tf_op | source)
XLA Modules:
  0.0 249.5 jit_solution(8012935296902372771)
XLA Ops:
  0.0 3.0 %copy.42 = f32[8,2,128,128]{3,1,0,2:T(2,128)} copy(f32[8,2,128,128]{3,2,1,0:T(8,128)} %bitcast.73) | data formatting | bytes 2097152 | tf_op jit(solution)/shard_map/reshape | solution.py:54
  3.0 7.5 %all-to-all-start.1 = ((f32[8,2,128,128]{3,1,0,2:T(2,128)}), f32[8,2,128,128]{3,1,0,2:T(2,128)S(1)}, u32[]{:S(2)}, u32[]{:S(2)}) async-start(f32[8,2,128,128]{3,1,0,2:T(2,128)} %copy.42), calls=%async_computation.1 | async-start | bytes 2097152 | tf_op jit(solution)/shard_map/all_to_all | solution.py:53
  10.5 0.0 copy-start.6
  10.5 0.7 copy-done.5
  11.2 34.0 %all-gather = f32[8,8,3]{1,2,0:T(4,128)S(1)} all-gather(f32[1,8,3]{1,2,0:T(4,128)S(1)} %fusion.25), channel_id=1, replica_groups=mesh['tm'=8,'azim'=32] {'tm'}, dimensions={0}, use_global_device_ids=true | all-gather | bytes 864 | tf_op jit(solution)/shard_map/all_gather | solution.py:68
  45.2 0.1 reshape.210
  45.3 0.3 copy.43
  45.7 1.8 fusion
  47.5 0.0 copy-start.1
  47.5 0.1 slice_bitcast_fusion.2
  47.6 5.6 %collective-permute-start = (f32[64,16,128]{2,0,1:T(8,128)S(1)}, f32[64,16,128]{2,0,1:T(8,128)S(1)}, u32[]{:S(2)}, u32[]{:S(2)}) collective-permute-start(f32[64,16,128]{2,0,1:T(8,128)S(1)} %get-tuple-element.22), channel_id=1, source_target_pairs={{0,1},{1,2},{2,3},{3,4},{4,5},{5,6},{6,7},{7,8},{8,9},{9,10},{10,1... | collective-permute-start | bytes 1572872 | tf_op jit(solution)/shard_map/ppermute | solution.py:16
  53.2 6.9 %collective-permute-start.7 = (f32[64,16,128]{2,0,1:T(8,128)S(1)}, f32[64,16,128]{2,0,1:T(8,128)S(1)}, u32[]{:S(2)}, u32[]{:S(2)}) collective-permute-start(f32[64,16,128]{2,0,1:T(8,128)S(1)} %get-tuple-element.23), channel_id=1, source_target_pairs={{0,16},{1,17},{2,18},{3,19},{4,20},{5,21},{6,22},{7,23},{8,24},{9,... | collective-permute-start | bytes 1572872 | tf_op jit(solution)/shard_map/ppermute | solution.py:16
  60.2 0.0 copy-start.2
  60.2 0.6 gather_fusion
  60.8 0.1 copy-done.2
  60.9 0.6 gather_fusion.1
  61.5 0.1 broadcast_select_fusion.11
  61.6 0.4 fusion.14
  61.9 0.0 collective-permute-done
  62.0 12.7 %collective-permute-done.7 = f32[64,16,128]{2,0,1:T(8,128)S(1)} collective-permute-done((f32[64,16,128]{2,0,1:T(8,128)S(1)}, f32[64,16,128]{2,0,1:T(8,128)S(1)}, u32[]{:S(2)}, u32[]{:S(2)}) %collective-permute-start.7) | collective-permute-done | bytes 524320 | tf_op jit(solution)/shard_map/ppermute | solution.py:16
  74.7 0.2 broadcast_select_fusion.5
  74.9 7.1 %collective-permute-start.1 = (f32[64,16,128]{2,0,1:T(8,128)S(1)}, f32[64,16,128]{2,0,1:T(8,128)S(1)}, u32[]{:S(2)}, u32[]{:S(2)}) collective-permute-start(f32[64,16,128]{2,0,1:T(8,128)S(1)} %get-tuple-element.20), channel_id=1, source_target_pairs={{0,2},{1,3},{2,4},{3,5},{4,6},{5,7},{6,8},{7,9},{8,10},{9,11},{10,... | collective-permute-start | bytes 1572872 | tf_op jit(solution)/shard_map/ppermute | solution.py:16
  82.0 9.7 %collective-permute-start.8 = (f32[64,16,128]{2,0,1:T(8,128)S(1)}, f32[64,16,128]{2,0,1:T(8,128)S(1)}, u32[]{:S(2)}, u32[]{:S(2)}) collective-permute-start(f32[64,16,128]{2,0,1:T(8,128)S(1)} %get-tuple-element.21), channel_id=1, source_target_pairs={{0,8},{1,9},{2,10},{3,11},{4,12},{5,13},{6,14},{7,15},{8,16},{9,17... | collective-permute-start | bytes 1572872 | tf_op jit(solution)/shard_map/ppermute | solution.py:16
  91.7 8.9 %collective-permute-done.1 = f32[64,16,128]{2,0,1:T(8,128)S(1)} collective-permute-done((f32[64,16,128]{2,0,1:T(8,128)S(1)}, f32[64,16,128]{2,0,1:T(8,128)S(1)}, u32[]{:S(2)}, u32[]{:S(2)}) %collective-permute-start.1) | collective-permute-done | bytes 524320 | tf_op jit(solution)/shard_map/ppermute | solution.py:16
  100.6 0.1 broadcast_select_fusion.6
  100.7 1.0 collective-permute-start.2
  101.8 11.3 %collective-permute-done.8 = f32[64,16,128]{2,0,1:T(8,128)S(1)} collective-permute-done((f32[64,16,128]{2,0,1:T(8,128)S(1)}, f32[64,16,128]{2,0,1:T(8,128)S(1)}, u32[]{:S(2)}, u32[]{:S(2)}) %collective-permute-start.8) | collective-permute-done | bytes 524320 | tf_op jit(solution)/shard_map/ppermute | solution.py:16
  113.1 0.1 broadcast_select_fusion.1
  113.2 0.1 collective-permute-start.9
  113.3 11.0 %collective-permute-done.2 = f32[64,16,128]{2,0,1:T(8,128)S(1)} collective-permute-done((f32[64,16,128]{2,0,1:T(8,128)S(1)}, f32[64,16,128]{2,0,1:T(8,128)S(1)}, u32[]{:S(2)}, u32[]{:S(2)}) %collective-permute-start.2) | collective-permute-done | bytes 524320 | tf_op jit(solution)/shard_map/ppermute | solution.py:16
  124.3 0.1 broadcast_select_fusion.7
  124.4 1.0 collective-permute-start.3
  125.4 1.0 collective-permute-done.9
  126.4 0.1 broadcast_select_fusion.2
  126.5 10.6 %collective-permute-start.10 = (f32[64,16,128]{2,0,1:T(8,128)S(1)}, f32[64,16,128]{2,0,1:T(8,128)S(1)}, u32[]{:S(2)}, u32[]{:S(2)}) collective-permute-start(f32[64,16,128]{2,0,1:T(8,128)S(1)} %broadcast_select_fusion.2), channel_id=1, source_target_pairs={{0,2},{1,3},{2,4},{3,5},{4,6},{5,7},{6,8},{7,9},{8,10},{9,11},{10,... | collective-permute-start | bytes 1572872 | tf_op jit(solution)/shard_map/ppermute | solution.py:16
  137.1 12.8 %collective-permute-done.3 = f32[64,16,128]{2,0,1:T(8,128)S(1)} collective-permute-done((f32[64,16,128]{2,0,1:T(8,128)S(1)}, f32[64,16,128]{2,0,1:T(8,128)S(1)}, u32[]{:S(2)}, u32[]{:S(2)}) %collective-permute-start.3) | collective-permute-done | bytes 524320 | tf_op jit(solution)/shard_map/ppermute | solution.py:16
  149.9 0.1 broadcast_select_fusion.8
  150.0 0.0 copy-start.4
  150.0 2.1 collective-permute-start.4
  152.1 0.1 broadcast_select_fusion.3
  152.3 26.2 %collective-permute-start.11 = (f32[64,16,128]{2,0,1:T(8,128)S(1)}, f32[64,16,128]{2,0,1:T(8,128)}, u32[]{:S(2)}, u32[]{:S(2)}) collective-permute-start(f32[64,16,128]{2,0,1:T(8,128)S(1)} %broadcast_select_fusion.3), channel_id=1, source_target_pairs={{0,1},{1,2},{2,3},{3,4},{4,5},{5,6},{6,7},{7,8},{8,9},{9,10},{10,1... | collective-permute-start | bytes 1572872 | tf_op jit(solution)/shard_map/ppermute | solution.py:16
  178.5 1.8 copy.37
  180.3 3.6 %all-to-all-start = ((f32[8,2,128,128]{3,1,0,2:T(2,128)}), f32[8,2,128,128]{3,1,0,2:T(2,128)S(1)}, u32[]{:S(2)}, u32[]{:S(2)}) async-start(f32[8,2,128,128]{3,1,0,2:T(2,128)} %copy.37), calls=%async_computation | async-start | bytes 2097152 | tf_op jit(solution)/shard_map/all_to_all | solution.py:60
  183.9 0.0 collective-permute-done.4
  183.9 0.1 broadcast_select_fusion.9
  184.0 1.7 collective-permute-start.5
  185.7 7.0 %collective-permute-start.6 = (f32[64,16,128]{2,0,1:T(8,128)S(1)}, f32[64,16,128]{2,0,1:T(8,128)}, u32[]{:S(2)}, u32[]{:S(2)}) collective-permute-start(f32[64,16,128]{2,0,1:T(8,128)S(1)} %broadcast_select_fusion.9), channel_id=1, source_target_pairs={{0,1},{1,2},{2,3},{3,4},{4,5},{5,6},{6,7},{7,8},{8,9},{9,10},{10,1... | collective-permute-start | bytes 1572872 | tf_op jit(solution)/shard_map/ppermute | solution.py:16
  192.7 1.3 collective-permute-done.11
  194.0 1.2 broadcast_select_fusion.4
  195.1 5.5 %collective-permute-start.12 = (f32[64,16,128]{2,0,1:T(8,128)S(1)}, f32[64,16,128]{2,0,1:T(8,128)S(1)}, u32[]{:S(2)}, u32[]{:S(2)}) collective-permute-start(f32[64,16,128]{2,0,1:T(8,128)S(1)} %broadcast_select_fusion.4), channel_id=1, source_target_pairs={{0,31},{1,0},{2,1},{3,2},{4,3},{5,4},{6,5},{7,6},{8,7},{9,8},{10,9... | collective-permute-start | bytes 1572872 | tf_op jit(solution)/shard_map/ppermute | solution.py:16
  200.6 5.0 %all-to-all-done = f32[8,2,128,128]{3,1,0,2:T(2,128)S(1)} async-done(((f32[8,2,128,128]{3,1,0,2:T(2,128)}), f32[8,2,128,128]{3,1,0,2:T(2,128)S(1)}, u32[]{:S(2)}, u32[]{:S(2)}) %all-to-all-start) | async-done | bytes 1048608 | tf_op jit(solution)/shard_map/all_to_all | solution.py:60
  205.7 0.3 copy.38
  206.0 0.6 copy.61
  206.6 9.3 %collective-permute-done.5 = f32[64,16,128]{2,0,1:T(8,128)S(1)} collective-permute-done((f32[64,16,128]{2,0,1:T(8,128)S(1)}, f32[64,16,128]{2,0,1:T(8,128)S(1)}, u32[]{:S(2)}, u32[]{:S(2)}) %collective-permute-start.5) | collective-permute-done | bytes 524320 | tf_op jit(solution)/shard_map/ppermute | solution.py:16
  215.9 10.1 %collective-permute-done.12 = f32[64,16,128]{2,0,1:T(8,128)S(1)} collective-permute-done((f32[64,16,128]{2,0,1:T(8,128)S(1)}, f32[64,16,128]{2,0,1:T(8,128)S(1)}, u32[]{:S(2)}, u32[]{:S(2)}) %collective-permute-start.12) | collective-permute-done | bytes 524320 | tf_op jit(solution)/shard_map/ppermute | solution.py:16
  226.0 1.7 add_bitcast_fusion.1
  227.7 0.1 multiply_reduce_fusion
  227.8 0.1 fusion.6
  227.9 1.2 fusion.3
  229.2 0.6 copy.46
  229.8 16.5 %all_to_all.51 = f32[64,2,16,128]{3,2,1,0:T(8,128)S(1)} all-to-all(f32[64,2,16,128]{3,2,1,0:T(8,128)S(1)} %copy.46), channel_id=1, replica_groups=mesh['tm'=8,'azim'=32] {'tm'}, dimensions={0} | all-to-all | bytes 2097152 | tf_op jit(solution)/shard_map/all_to_all | solution.py:97
  246.2 0.1 copy.47
  246.3 1.1 copy-done.3
  247.5 2.1 sub.12
  (20 shorter events, 0.1 us)
Async XLA Ops:
  0.0 200.6 %copy-start = (f32[1,16384]{1,0:T(1,128)S(1)}, f32[1,16384]{1,0:T(1,128)}, u32[]{:S(2)}) copy-start(f32[1,16384]{1,0:T(1,128)} %param.14) | copy-start | bytes 196612
  3.0 42.3 %all-to-all-start.1 = ((f32[8,2,128,128]{3,1,0,2:T(2,128)}), f32[8,2,128,128]{3,1,0,2:T(2,128)S(1)}, u32[]{:S(2)}, u32[]{:S(2)}) async-start(f32[8,2,128,128]{3,1,0,2:T(2,128)} %copy.42), calls=%async_computation.1 | async-start | bytes 2097152 | tf_op jit(solution)/shard_map/all_to_all | solution.py:53
  10.5 0.7 copy-start.5
  10.5 0.7 copy-start.6
  47.5 12.7 %copy-start.1 = (s32[32,5]{1,0:T(8,128)S(1)}, s32[32,5]{1,0:T(8,128)}, u32[]{:S(2)}) copy-start(s32[32,5]{1,0:T(8,128)} %constant.99.clone2.1) | copy-start | bytes 1924
  47.6 14.4 %collective-permute-start = (f32[64,16,128]{2,0,1:T(8,128)S(1)}, f32[64,16,128]{2,0,1:T(8,128)S(1)}, u32[]{:S(2)}, u32[]{:S(2)}) collective-permute-start(f32[64,16,128]{2,0,1:T(8,128)S(1)} %get-tuple-element.22), channel_id=1, source_target_pairs={{0,1},{1,2},{2,3},{3,4},{4,5},{5,6},{6,7},{7,8},{8,9},{9,10},{10,1... | collective-permute-start | bytes 1572872 | tf_op jit(solution)/shard_map/ppermute | solution.py:16
  53.2 21.5 %collective-permute-start.7 = (f32[64,16,128]{2,0,1:T(8,128)S(1)}, f32[64,16,128]{2,0,1:T(8,128)S(1)}, u32[]{:S(2)}, u32[]{:S(2)}) collective-permute-start(f32[64,16,128]{2,0,1:T(8,128)S(1)} %get-tuple-element.23), channel_id=1, source_target_pairs={{0,16},{1,17},{2,18},{3,19},{4,20},{5,21},{6,22},{7,23},{8,24},{9,... | collective-permute-start | bytes 1572872 | tf_op jit(solution)/shard_map/ppermute | solution.py:16
  60.2 0.7 copy-start.2
  74.9 25.7 %collective-permute-start.1 = (f32[64,16,128]{2,0,1:T(8,128)S(1)}, f32[64,16,128]{2,0,1:T(8,128)S(1)}, u32[]{:S(2)}, u32[]{:S(2)}) collective-permute-start(f32[64,16,128]{2,0,1:T(8,128)S(1)} %get-tuple-element.20), channel_id=1, source_target_pairs={{0,2},{1,3},{2,4},{3,5},{4,6},{5,7},{6,8},{7,9},{8,10},{9,11},{10,... | collective-permute-start | bytes 1572872 | tf_op jit(solution)/shard_map/ppermute | solution.py:16
  82.0 31.1 %collective-permute-start.8 = (f32[64,16,128]{2,0,1:T(8,128)S(1)}, f32[64,16,128]{2,0,1:T(8,128)S(1)}, u32[]{:S(2)}, u32[]{:S(2)}) collective-permute-start(f32[64,16,128]{2,0,1:T(8,128)S(1)} %get-tuple-element.21), channel_id=1, source_target_pairs={{0,8},{1,9},{2,10},{3,11},{4,12},{5,13},{6,14},{7,15},{8,16},{9,17... | collective-permute-start | bytes 1572872 | tf_op jit(solution)/shard_map/ppermute | solution.py:16
  100.7 23.6 %collective-permute-start.2 = (f32[64,16,128]{2,0,1:T(8,128)S(1)}, f32[64,16,128]{2,0,1:T(8,128)S(1)}, u32[]{:S(2)}, u32[]{:S(2)}) collective-permute-start(f32[64,16,128]{2,0,1:T(8,128)S(1)} %broadcast_select_fusion.6), channel_id=1, source_target_pairs={{0,4},{1,5},{2,6},{3,7},{4,8},{5,9},{6,10},{7,11},{8,12},{9,13},{1... | collective-permute-start | bytes 1572872 | tf_op jit(solution)/shard_map/ppermute | solution.py:16
  113.2 13.1 %collective-permute-start.9 = (f32[64,16,128]{2,0,1:T(8,128)S(1)}, f32[64,16,128]{2,0,1:T(8,128)S(1)}, u32[]{:S(2)}, u32[]{:S(2)}) collective-permute-start(f32[64,16,128]{2,0,1:T(8,128)S(1)} %broadcast_select_fusion.1), channel_id=1, source_target_pairs={{0,28},{1,29},{2,30},{3,31},{4,0},{5,1},{6,2},{7,3},{8,4},{9,5},{1... | collective-permute-start | bytes 1572872 | tf_op jit(solution)/shard_map/ppermute | solution.py:16
  124.4 25.5 %collective-permute-start.3 = (f32[64,16,128]{2,0,1:T(8,128)S(1)}, f32[64,16,128]{2,0,1:T(8,128)S(1)}, u32[]{:S(2)}, u32[]{:S(2)}) collective-permute-start(f32[64,16,128]{2,0,1:T(8,128)S(1)} %broadcast_select_fusion.7), channel_id=1, source_target_pairs={{0,24},{1,25},{2,26},{3,27},{4,28},{5,29},{6,30},{7,31},{8,0},{9,1... | collective-permute-start | bytes 1572872 | tf_op jit(solution)/shard_map/ppermute | solution.py:16
  126.5 25.6 %collective-permute-start.10 = (f32[64,16,128]{2,0,1:T(8,128)S(1)}, f32[64,16,128]{2,0,1:T(8,128)S(1)}, u32[]{:S(2)}, u32[]{:S(2)}) collective-permute-start(f32[64,16,128]{2,0,1:T(8,128)S(1)} %broadcast_select_fusion.2), channel_id=1, source_target_pairs={{0,2},{1,3},{2,4},{3,5},{4,6},{5,7},{6,8},{7,9},{8,10},{9,11},{10,... | collective-permute-start | bytes 1572872 | tf_op jit(solution)/shard_map/ppermute | solution.py:16
  150.0 28.5 %copy-start.4 = (f32[8,2,1,16384]{3,2,1,0:T(1,128)S(1)}, f32[8,2,1,16384]{3,2,1,0:T(1,128)}, u32[]{:S(2)}) copy-start(f32[8,2,1,16384]{3,2,1,0:T(1,128)} %param.11) | copy-start | bytes 3145732
  150.0 33.8 %collective-permute-start.4 = (f32[64,16,128]{2,0,1:T(8,128)S(1)}, f32[64,16,128]{2,0,1:T(8,128)S(1)}, u32[]{:S(2)}, u32[]{:S(2)}) collective-permute-start(f32[64,16,128]{2,0,1:T(8,128)S(1)} %broadcast_select_fusion.8), channel_id=1, source_target_pairs={{0,16},{1,17},{2,18},{3,19},{4,20},{5,21},{6,22},{7,23},{8,24},{9,... | collective-permute-start | bytes 1572872 | tf_op jit(solution)/shard_map/ppermute | solution.py:16
  152.3 41.7 %collective-permute-start.11 = (f32[64,16,128]{2,0,1:T(8,128)S(1)}, f32[64,16,128]{2,0,1:T(8,128)}, u32[]{:S(2)}, u32[]{:S(2)}) collective-permute-start(f32[64,16,128]{2,0,1:T(8,128)S(1)} %broadcast_select_fusion.3), channel_id=1, source_target_pairs={{0,1},{1,2},{2,3},{3,4},{4,5},{5,6},{6,7},{7,8},{8,9},{9,10},{10,1... | collective-permute-start | bytes 1572872 | tf_op jit(solution)/shard_map/ppermute | solution.py:16
  180.3 25.4 %all-to-all-start = ((f32[8,2,128,128]{3,1,0,2:T(2,128)}), f32[8,2,128,128]{3,1,0,2:T(2,128)S(1)}, u32[]{:S(2)}, u32[]{:S(2)}) async-start(f32[8,2,128,128]{3,1,0,2:T(2,128)} %copy.37), calls=%async_computation | async-start | bytes 2097152 | tf_op jit(solution)/shard_map/all_to_all | solution.py:60
  184.0 31.9 %collective-permute-start.5 = (f32[64,16,128]{2,0,1:T(8,128)S(1)}, f32[64,16,128]{2,0,1:T(8,128)S(1)}, u32[]{:S(2)}, u32[]{:S(2)}) collective-permute-start(f32[64,16,128]{2,0,1:T(8,128)S(1)} %broadcast_select_fusion.9), channel_id=1, source_target_pairs={{0,31},{1,0},{2,1},{3,2},{4,3},{5,4},{6,5},{7,6},{8,7},{9,8},{10,9... | collective-permute-start | bytes 1572872 | tf_op jit(solution)/shard_map/ppermute | solution.py:16
  185.7 30.2 %collective-permute-start.6 = (f32[64,16,128]{2,0,1:T(8,128)S(1)}, f32[64,16,128]{2,0,1:T(8,128)}, u32[]{:S(2)}, u32[]{:S(2)}) collective-permute-start(f32[64,16,128]{2,0,1:T(8,128)S(1)} %broadcast_select_fusion.9), channel_id=1, source_target_pairs={{0,1},{1,2},{2,3},{3,4},{4,5},{5,6},{6,7},{7,8},{8,9},{9,10},{10,1... | collective-permute-start | bytes 1572872 | tf_op jit(solution)/shard_map/ppermute | solution.py:16
  195.1 30.9 %collective-permute-start.12 = (f32[64,16,128]{2,0,1:T(8,128)S(1)}, f32[64,16,128]{2,0,1:T(8,128)S(1)}, u32[]{:S(2)}, u32[]{:S(2)}) collective-permute-start(f32[64,16,128]{2,0,1:T(8,128)S(1)} %broadcast_select_fusion.4), channel_id=1, source_target_pairs={{0,31},{1,0},{2,1},{3,2},{4,3},{5,4},{6,5},{7,6},{8,7},{9,8},{10,9... | collective-permute-start | bytes 1572872 | tf_op jit(solution)/shard_map/ppermute | solution.py:16
  200.6 25.4 %collective-permute-start.13 = (f32[64,16,128]{2,0,1:T(8,128)S(1)}, f32[64,16,128]{2,0,1:T(8,128)}, u32[]{:S(2)}, u32[]{:S(2)}) collective-permute-start(f32[64,16,128]{2,0,1:T(8,128)S(1)} %broadcast_select_fusion.4), channel_id=1, source_target_pairs={{0,1},{1,2},{2,3},{3,4},{4,5},{5,6},{6,7},{7,8},{8,9},{9,10},{10,1... | collective-permute-start | bytes 1572872 | tf_op jit(solution)/shard_map/ppermute | solution.py:16
  246.2 1.2 copy-start.3
where the time goes:
time: 250 us
  starting transfers between devices  95.6 us (38%)
  waiting for transfers between devices  83.4 us (33%)
  blocking collectives  50.5 us (20%)
  local copies, waits for them, and re-layouts  10.1 us (4%)
  other arithmetic  6.77 us (3%)
  matrix products  2.96 us (1%)
    ppermute x14, starting transfers between devices, shifted(): return lax.ppermute(value, axis, pairs)  84.5 us
    ppermute x14, waiting for transfers between devices, shifted(): return lax.ppermute(value, axis, pairs)  78.3 us
    all_gather x1, blocking collectives, body(): small = lax.all_gather(small, 'tm', tiled=True).astype(jnp.int32)  34 us
    all_to_all x1, blocking collectives, body(): lax.all_to_all(summed, 'tm', split_axis=0, concat_axis=2, tiled=True)  16.5 us
    all_to_all x1, starting transfers between devices, body(): lax.all_to_all(rotor_coeffs.reshape(local_c, comp, rows, LANES), 'tm', sp...  7.48 us
    all_to_all x1, waiting for transfers between devices, body(): lax.all_to_all(mortar_weights.reshape(local_j, sten, rows, LANES), 'tm',...  5.02 us
  transfers between devices with their start and end apart: 16, of which 10 were waited for; matrix products, arithmetic and copies ran while one was open for 3% of the time, Pallas kernels for 0%

commit v1 on v0

--- a/solution.py
+++ b/solution.py
@@ -4,6 +4,7 @@
 import numpy as np
 from jax import lax
 from jax.sharding import PartitionSpec as P
+from jax.lax import all_to_all, axis_size
 
 KC = 64
 NT = 64
@@ -65,7 +66,13 @@
         tiled=True,
     )
     small = jnp.concatenate([block_shifts[:, None], stencil_offsets], axis=1).astype(jnp.float32)
-    small = lax.all_gather(small, "tm", tiled=True).astype(jnp.int32)
+
+    def _plan_arrays(slab_in, dim_k):
+        y_new = all_to_all(jnp.stack([slab_in] * axis_size("tm"), 0), "tm", 0, 0)
+        n_now = jnp.concatenate(y_new, dim_k)
+        return n_now
+
+    small = _plan_arrays(small, 0).astype(jnp.int32)
     shifts, offsets = (small[:, 0], small[:, 1:])
     gain = lax.dynamic_slice_in_dim(
         reluctivity.reshape(rows, LANES), lax.axis_index("tm") * chunk, chunk, axis=0

time: 250 us -> 237 us (0.948)
  blocking collectives: 50.5 us -> 18.2 us
  waiting for transfers between devices: 83.4 us -> 99 us
  starting transfers between devices: 95.6 us -> 98.2 us
    all_gather x1 -> x0, blocking collectives: 34 us -> none  [body(): small = lax.all_gather(small, 'tm', tiled=True).astype(jnp.int32)]
    all_to_all x1, waiting for transfers between devices: 0.01 us -> 12.8 us  [body(): lax.all_to_all(rotor_coeffs.reshape(local_c, comp, rows, LANES), 'tm', sp...]
    all_to_all x0 -> x1, starting transfers between devices: none -> 7.48 us  [_plan_arrays(): y_new = all_to_all(jnp.stack([slab_in] * axis_size('tm'), 0), 'tm', 0, 0)]
    all_to_all x1, starting transfers between devices: 7.48 us -> 3.56 us  [body(): lax.all_to_all(rotor_coeffs.reshape(local_c, comp, rows, LANES), 'tm', sp...]
    all_to_all x0 -> x1, waiting for transfers between devices: none -> 3.57 us  [_plan_arrays(): y_new = all_to_all(jnp.stack([slab_in] * axis_size('tm'), 0), 'tm', 0, 0)]
  transfers between devices with their start and end apart: 16 -> 17, of which waited for: 10 -> 12; matrix products, arithmetic and copies ran while one was open for 3% -> 4% of each run, Pallas kernels for 0% -> 0%
where the time goes in v1:
time: 237 us; the launch traced here: 236 us
  waiting for transfers between devices  99 us (42%)
  starting transfers between devices  98.2 us (41%)
  blocking collectives  18.2 us (8%)
  local copies, waits for them, and re-layouts  10.7 us (5%)
  other arithmetic  6.77 us (3%)
  matrix products  2.96 us (1%)
    ppermute x14, starting transfers between devices, shifted(): return lax.ppermute(value, axis, pairs)  83.6 us
    ppermute x14, waiting for transfers between devices, shifted(): return lax.ppermute(value, axis, pairs)  77.6 us
    all_to_all x1, blocking collectives, body(): lax.all_to_all(summed, 'tm', split_axis=0, concat_axis=2, tiled=True)  18.2 us
    all_to_all x1, waiting for transfers between devices, body(): lax.all_to_all(rotor_coeffs.reshape(local_c, comp, rows, LANES), 'tm', sp...  12.8 us
    all_to_all x1, starting transfers between devices, _plan_arrays(): y_new = all_to_all(jnp.stack([slab_in] * axis_size('tm'), 0), 'tm', 0, 0)  7.48 us
    all_to_all x1, waiting for transfers between devices, body(): lax.all_to_all(mortar_weights.reshape(local_j, sten, rows, LANES), 'tm',...  5.04 us
  transfers between devices with their start and end apart: 17, of which 12 were waited for; matrix products, arithmetic and copies ran while one was open for 4% of the time, Pallas kernels for 0%

profile of v1, /device:TPU:1, one launch (start us, length us, event | category | flops | bytes accessed | tf_op | source)
XLA Modules:
  0.0 236.2 jit_solution(2325139877974604203)
XLA Ops:
  0.0 0.7 copy-done.5
  0.7 0.6 stack.8
  1.3 7.5 %all-to-all-start.1 = ((f32[8,8,3]{1,2,0:T(4,128)}), f32[8,8,3]{1,2,0:T(4,128)S(1)}, u32[]{:S(2)}, u32[]{:S(2)}) async-start(f32[8,8,3]{1,2,0:T(4,128)} %stack.8), calls=%async_computation.1 | async-start | bytes 32768 | tf_op jit(solution)/shard_map/all_to_all | solution.py:71
  8.8 3.0 %copy.40 = f32[8,2,128,128]{3,1,0,2:T(2,128)} copy(f32[8,2,128,128]{3,2,1,0:T(8,128)} %bitcast.71) | data formatting | bytes 2097152 | tf_op jit(solution)/shard_map/reshape | solution.py:55
  11.8 3.6 %all-to-all-done.1 = f32[8,8,3]{1,2,0:T(4,128)S(1)} async-done(((f32[8,8,3]{1,2,0:T(4,128)}), f32[8,8,3]{1,2,0:T(4,128)S(1)}, u32[]{:S(2)}, u32[]{:S(2)}) %all-to-all-start.1) | async-done | bytes 800 | tf_op jit(solution)/shard_map/all_to_all | solution.py:71
  15.4 3.6 %all-to-all-start.2 = ((f32[8,2,128,128]{3,1,0,2:T(2,128)}), f32[8,2,128,128]{3,1,0,2:T(2,128)S(1)}, u32[]{:S(2)}, u32[]{:S(2)}) async-start(f32[8,2,128,128]{3,1,0,2:T(2,128)} %copy.40), calls=%async_computation.2 | async-start | bytes 2097152 | tf_op jit(solution)/shard_map/all_to_all | solution.py:54
  19.0 0.1 convert_element_type.19
  19.1 12.8 %all-to-all-done.2 = f32[8,2,128,128]{3,1,0,2:T(2,128)S(1)} async-done(((f32[8,2,128,128]{3,1,0,2:T(2,128)}), f32[8,2,128,128]{3,1,0,2:T(2,128)S(1)}, u32[]{:S(2)}, u32[]{:S(2)}) %all-to-all-start.2) | async-done | bytes 1048608 | tf_op jit(solution)/shard_map/all_to_all | solution.py:54
  31.9 0.3 copy.41
  32.2 1.8 fusion
  34.0 0.0 copy-start.1
  34.0 0.1 slice_bitcast_fusion.2
  34.1 4.1 %collective-permute-start = (f32[64,16,128]{2,0,1:T(8,128)S(1)}, f32[64,16,128]{2,0,1:T(8,128)S(1)}, u32[]{:S(2)}, u32[]{:S(2)}) collective-permute-start(f32[64,16,128]{2,0,1:T(8,128)S(1)} %get-tuple-element.22), channel_id=1, source_target_pairs={{0,1},{1,2},{2,3},{3,4},{4,5},{5,6},{6,7},{7,8},{8,9},{9,10},{10,1... | collective-permute-start | bytes 1572872 | tf_op jit(solution)/shard_map/ppermute | solution.py:17
  38.2 6.9 %collective-permute-start.7 = (f32[64,16,128]{2,0,1:T(8,128)S(1)}, f32[64,16,128]{2,0,1:T(8,128)S(1)}, u32[]{:S(2)}, u32[]{:S(2)}) collective-permute-start(f32[64,16,128]{2,0,1:T(8,128)S(1)} %get-tuple-element.23), channel_id=1, source_target_pairs={{0,16},{1,17},{2,18},{3,19},{4,20},{5,21},{6,22},{7,23},{8,24},{9,... | collective-permute-start | bytes 1572872 | tf_op jit(solution)/shard_map/ppermute | solution.py:17
  45.2 0.0 copy-start.2
  45.2 0.6 gather_fusion
  45.8 0.1 copy-done.2
  45.9 0.6 gather_fusion.1
  46.5 0.1 broadcast_select_fusion.11
  46.6 0.4 fusion.14
  47.0 12.8 %collective-permute-done.7 = f32[64,16,128]{2,0,1:T(8,128)S(1)} collective-permute-done((f32[64,16,128]{2,0,1:T(8,128)S(1)}, f32[64,16,128]{2,0,1:T(8,128)S(1)}, u32[]{:S(2)}, u32[]{:S(2)}) %collective-permute-start.7) | collective-permute-done | bytes 524320 | tf_op jit(solution)/shard_map/ppermute | solution.py:17
  59.7 0.2 broadcast_select_fusion.5
  59.9 7.1 %collective-permute-start.1 = (f32[64,16,128]{2,0,1:T(8,128)S(1)}, f32[64,16,128]{2,0,1:T(8,128)S(1)}, u32[]{:S(2)}, u32[]{:S(2)}) collective-permute-start(f32[64,16,128]{2,0,1:T(8,128)S(1)} %get-tuple-element.20), channel_id=1, source_target_pairs={{0,2},{1,3},{2,4},{3,5},{4,6},{5,7},{6,8},{7,9},{8,10},{9,11},{10,... | collective-permute-start | bytes 1572872 | tf_op jit(solution)/shard_map/ppermute | solution.py:17
  67.0 9.6 %collective-permute-start.8 = (f32[64,16,128]{2,0,1:T(8,128)S(1)}, f32[64,16,128]{2,0,1:T(8,128)S(1)}, u32[]{:S(2)}, u32[]{:S(2)}) collective-permute-start(f32[64,16,128]{2,0,1:T(8,128)S(1)} %get-tuple-element.21), channel_id=1, source_target_pairs={{0,8},{1,9},{2,10},{3,11},{4,12},{5,13},{6,14},{7,15},{8,16},{9,17... | collective-permute-start | bytes 1572872 | tf_op jit(solution)/shard_map/ppermute | solution.py:17
  76.7 8.9 %collective-permute-done.1 = f32[64,16,128]{2,0,1:T(8,128)S(1)} collective-permute-done((f32[64,16,128]{2,0,1:T(8,128)S(1)}, f32[64,16,128]{2,0,1:T(8,128)S(1)}, u32[]{:S(2)}, u32[]{:S(2)}) %collective-permute-start.1) | collective-permute-done | bytes 524320 | tf_op jit(solution)/shard_map/ppermute | solution.py:17
  85.6 0.1 broadcast_select_fusion.6
  85.7 1.1 collective-permute-start.2
  86.8 11.3 %collective-permute-done.8 = f32[64,16,128]{2,0,1:T(8,128)S(1)} collective-permute-done((f32[64,16,128]{2,0,1:T(8,128)S(1)}, f32[64,16,128]{2,0,1:T(8,128)S(1)}, u32[]{:S(2)}, u32[]{:S(2)}) %collective-permute-start.8) | collective-permute-done | bytes 524320 | tf_op jit(solution)/shard_map/ppermute | solution.py:17
  98.1 0.1 broadcast_select_fusion.1
  98.2 0.1 collective-permute-start.9
  98.3 11.0 %collective-permute-done.2 = f32[64,16,128]{2,0,1:T(8,128)S(1)} collective-permute-done((f32[64,16,128]{2,0,1:T(8,128)S(1)}, f32[64,16,128]{2,0,1:T(8,128)S(1)}, u32[]{:S(2)}, u32[]{:S(2)}) %collective-permute-start.2) | collective-permute-done | bytes 524320 | tf_op jit(solution)/shard_map/ppermute | solution.py:17
  109.3 0.1 broadcast_select_fusion.7
  109.4 1.0 collective-permute-start.3
  110.4 1.0 collective-permute-done.9
  111.4 0.1 broadcast_select_fusion.2
  111.5 10.6 %collective-permute-start.10 = (f32[64,16,128]{2,0,1:T(8,128)S(1)}, f32[64,16,128]{2,0,1:T(8,128)S(1)}, u32[]{:S(2)}, u32[]{:S(2)}) collective-permute-start(f32[64,16,128]{2,0,1:T(8,128)S(1)} %broadcast_select_fusion.2), channel_id=1, source_target_pairs={{0,2},{1,3},{2,4},{3,5},{4,6},{5,7},{6,8},{7,9},{8,10},{9,11},{10,... | collective-permute-start | bytes 1572872 | tf_op jit(solution)/shard_map/ppermute | solution.py:17
  122.1 12.8 %collective-permute-done.3 = f32[64,16,128]{2,0,1:T(8,128)S(1)} collective-permute-done((f32[64,16,128]{2,0,1:T(8,128)S(1)}, f32[64,16,128]{2,0,1:T(8,128)S(1)}, u32[]{:S(2)}, u32[]{:S(2)}) %collective-permute-start.3) | collective-permute-done | bytes 524320 | tf_op jit(solution)/shard_map/ppermute | solution.py:17
  134.9 0.1 broadcast_select_fusion.8
  135.0 0.0 copy-start.4
  135.1 2.0 collective-permute-start.4
  137.1 0.1 broadcast_select_fusion.3
  137.2 26.1 %collective-permute-start.11 = (f32[64,16,128]{2,0,1:T(8,128)S(1)}, f32[64,16,128]{2,0,1:T(8,128)}, u32[]{:S(2)}, u32[]{:S(2)}) collective-permute-start(f32[64,16,128]{2,0,1:T(8,128)S(1)} %broadcast_select_fusion.3), channel_id=1, source_target_pairs={{0,1},{1,2},{2,3},{3,4},{4,5},{5,6},{6,7},{7,8},{8,9},{9,10},{10,1... | collective-permute-start | bytes 1572872 | tf_op jit(solution)/shard_map/ppermute | solution.py:17
  163.3 1.8 copy.35
  165.1 3.6 %all-to-all-start = ((f32[8,2,128,128]{3,1,0,2:T(2,128)}), f32[8,2,128,128]{3,1,0,2:T(2,128)S(1)}, u32[]{:S(2)}, u32[]{:S(2)}) async-start(f32[8,2,128,128]{3,1,0,2:T(2,128)} %copy.35), calls=%async_computation | async-start | bytes 2097152 | tf_op jit(solution)/shard_map/all_to_all | solution.py:61
  168.7 0.1 broadcast_select_fusion.9
  168.8 1.8 collective-permute-start.5
  170.7 6.9 %collective-permute-start.6 = (f32[64,16,128]{2,0,1:T(8,128)S(1)}, f32[64,16,128]{2,0,1:T(8,128)}, u32[]{:S(2)}, u32[]{:S(2)}) collective-permute-start(f32[64,16,128]{2,0,1:T(8,128)S(1)} %broadcast_select_fusion.9), channel_id=1, source_target_pairs={{0,1},{1,2},{2,3},{3,4},{4,5},{5,6},{6,7},{7,8},{8,9},{9,10},{10,1... | collective-permute-start | bytes 1572872 | tf_op jit(solution)/shard_map/ppermute | solution.py:17
  177.5 0.6 collective-permute-done.11
  178.1 1.2 broadcast_select_fusion.4
  179.3 6.3 %collective-permute-start.12 = (f32[64,16,128]{2,0,1:T(8,128)S(1)}, f32[64,16,128]{2,0,1:T(8,128)S(1)}, u32[]{:S(2)}, u32[]{:S(2)}) collective-permute-start(f32[64,16,128]{2,0,1:T(8,128)S(1)} %broadcast_select_fusion.4), channel_id=1, source_target_pairs={{0,31},{1,0},{2,1},{3,2},{4,3},{5,4},{6,5},{7,6},{8,7},{9,8},{10,9... | collective-permute-start | bytes 1572872 | tf_op jit(solution)/shard_map/ppermute | solution.py:17
  185.6 5.0 %all-to-all-done = f32[8,2,128,128]{3,1,0,2:T(2,128)S(1)} async-done(((f32[8,2,128,128]{3,1,0,2:T(2,128)}), f32[8,2,128,128]{3,1,0,2:T(2,128)S(1)}, u32[]{:S(2)}, u32[]{:S(2)}) %all-to-all-start) | async-done | bytes 1048608 | tf_op jit(solution)/shard_map/all_to_all | solution.py:61
  190.7 0.3 copy.36
  191.0 0.6 copy.59
  191.6 8.8 %collective-permute-done.5 = f32[64,16,128]{2,0,1:T(8,128)S(1)} collective-permute-done((f32[64,16,128]{2,0,1:T(8,128)S(1)}, f32[64,16,128]{2,0,1:T(8,128)S(1)}, u32[]{:S(2)}, u32[]{:S(2)}) %collective-permute-start.5) | collective-permute-done | bytes 524320 | tf_op jit(solution)/shard_map/ppermute | solution.py:17
  200.4 10.5 %collective-permute-done.12 = f32[64,16,128]{2,0,1:T(8,128)S(1)} collective-permute-done((f32[64,16,128]{2,0,1:T(8,128)S(1)}, f32[64,16,128]{2,0,1:T(8,128)S(1)}, u32[]{:S(2)}, u32[]{:S(2)}) %collective-permute-start.12) | collective-permute-done | bytes 524320 | tf_op jit(solution)/shard_map/ppermute | solution.py:17
  210.9 1.7 add_bitcast_fusion.1
  212.6 0.1 multiply_reduce_fusion
  212.7 0.1 fusion.6
  212.8 1.2 fusion.3
  214.0 0.6 copy.44
  214.7 18.2 %all_to_all.56 = f32[64,2,16,128]{3,2,1,0:T(8,128)S(1)} all-to-all(f32[64,2,16,128]{3,2,1,0:T(8,128)S(1)} %copy.44), channel_id=1, replica_groups=mesh['tm'=8,'azim'=32] {'tm'}, dimensions={0} | all-to-all | bytes 2097152 | tf_op jit(solution)/shard_map/all_to_all | solution.py:104
  232.9 0.1 copy.45
  233.0 1.1 copy-done.3
  234.1 2.1 sub.12
  (22 shorter events, 0.1 us)
Async XLA Ops:
  0.0 185.6 %copy-start = (f32[1,16384]{1,0:T(1,128)S(1)}, f32[1,16384]{1,0:T(1,128)}, u32[]{:S(2)}) copy-start(f32[1,16384]{1,0:T(1,128)} %param.14) | copy-start | bytes 196612
  0.0 0.7 copy-start.5
  0.0 0.7 copy-start.6
  1.3 14.1 %all-to-all-start.1 = ((f32[8,8,3]{1,2,0:T(4,128)}), f32[8,8,3]{1,2,0:T(4,128)S(1)}, u32[]{:S(2)}, u32[]{:S(2)}) async-start(f32[8,8,3]{1,2,0:T(4,128)} %stack.8), calls=%async_computation.1 | async-start | bytes 32768 | tf_op jit(solution)/shard_map/all_to_all | solution.py:71
  15.4 16.5 %all-to-all-start.2 = ((f32[8,2,128,128]{3,1,0,2:T(2,128)}), f32[8,2,128,128]{3,1,0,2:T(2,128)S(1)}, u32[]{:S(2)}, u32[]{:S(2)}) async-start(f32[8,2,128,128]{3,1,0,2:T(2,128)} %copy.40), calls=%async_computation.2 | async-start | bytes 2097152 | tf_op jit(solution)/shard_map/all_to_all | solution.py:54
  34.0 11.2 %copy-start.1 = (s32[32,5]{1,0:T(8,128)S(1)}, s32[32,5]{1,0:T(8,128)}, u32[]{:S(2)}) copy-start(s32[32,5]{1,0:T(8,128)} %constant.99.clone2.1) | copy-start | bytes 1924
  34.1 12.8 %collective-permute-start = (f32[64,16,128]{2,0,1:T(8,128)S(1)}, f32[64,16,128]{2,0,1:T(8,128)S(1)}, u32[]{:S(2)}, u32[]{:S(2)}) collective-permute-start(f32[64,16,128]{2,0,1:T(8,128)S(1)} %get-tuple-element.22), channel_id=1, source_target_pairs={{0,1},{1,2},{2,3},{3,4},{4,5},{5,6},{6,7},{7,8},{8,9},{9,10},{10,1... | collective-permute-start | bytes 1572872 | tf_op jit(solution)/shard_map/ppermute | solution.py:17
  38.2 21.5 %collective-permute-start.7 = (f32[64,16,128]{2,0,1:T(8,128)S(1)}, f32[64,16,128]{2,0,1:T(8,128)S(1)}, u32[]{:S(2)}, u32[]{:S(2)}) collective-permute-start(f32[64,16,128]{2,0,1:T(8,128)S(1)} %get-tuple-element.23), channel_id=1, source_target_pairs={{0,16},{1,17},{2,18},{3,19},{4,20},{5,21},{6,22},{7,23},{8,24},{9,... | collective-permute-start | bytes 1572872 | tf_op jit(solution)/shard_map/ppermute | solution.py:17
  45.2 0.7 copy-start.2
  59.9 25.6 %collective-permute-start.1 = (f32[64,16,128]{2,0,1:T(8,128)S(1)}, f32[64,16,128]{2,0,1:T(8,128)S(1)}, u32[]{:S(2)}, u32[]{:S(2)}) collective-permute-start(f32[64,16,128]{2,0,1:T(8,128)S(1)} %get-tuple-element.20), channel_id=1, source_target_pairs={{0,2},{1,3},{2,4},{3,5},{4,6},{5,7},{6,8},{7,9},{8,10},{9,11},{10,... | collective-permute-start | bytes 1572872 | tf_op jit(solution)/shard_map/ppermute | solution.py:17
  67.0 31.1 %collective-permute-start.8 = (f32[64,16,128]{2,0,1:T(8,128)S(1)}, f32[64,16,128]{2,0,1:T(8,128)S(1)}, u32[]{:S(2)}, u32[]{:S(2)}) collective-permute-start(f32[64,16,128]{2,0,1:T(8,128)S(1)} %get-tuple-element.21), channel_id=1, source_target_pairs={{0,8},{1,9},{2,10},{3,11},{4,12},{5,13},{6,14},{7,15},{8,16},{9,17... | collective-permute-start | bytes 1572872 | tf_op jit(solution)/shard_map/ppermute | solution.py:17
  85.7 23.6 %collective-permute-start.2 = (f32[64,16,128]{2,0,1:T(8,128)S(1)}, f32[64,16,128]{2,0,1:T(8,128)S(1)}, u32[]{:S(2)}, u32[]{:S(2)}) collective-permute-start(f32[64,16,128]{2,0,1:T(8,128)S(1)} %broadcast_select_fusion.6), channel_id=1, source_target_pairs={{0,4},{1,5},{2,6},{3,7},{4,8},{5,9},{6,10},{7,11},{8,12},{9,13},{1... | collective-permute-start | bytes 1572872 | tf_op jit(solution)/shard_map/ppermute | solution.py:17
  98.2 13.1 %collective-permute-start.9 = (f32[64,16,128]{2,0,1:T(8,128)S(1)}, f32[64,16,128]{2,0,1:T(8,128)S(1)}, u32[]{:S(2)}, u32[]{:S(2)}) collective-permute-start(f32[64,16,128]{2,0,1:T(8,128)S(1)} %broadcast_select_fusion.1), channel_id=1, source_target_pairs={{0,28},{1,29},{2,30},{3,31},{4,0},{5,1},{6,2},{7,3},{8,4},{9,5},{1... | collective-permute-start | bytes 1572872 | tf_op jit(solution)/shard_map/ppermute | solution.py:17
  109.4 25.5 %collective-permute-start.3 = (f32[64,16,128]{2,0,1:T(8,128)S(1)}, f32[64,16,128]{2,0,1:T(8,128)S(1)}, u32[]{:S(2)}, u32[]{:S(2)}) collective-permute-start(f32[64,16,128]{2,0,1:T(8,128)S(1)} %broadcast_select_fusion.7), channel_id=1, source_target_pairs={{0,24},{1,25},{2,26},{3,27},{4,28},{5,29},{6,30},{7,31},{8,0},{9,1... | collective-permute-start | bytes 1572872 | tf_op jit(solution)/shard_map/ppermute | solution.py:17
  111.5 25.6 %collective-permute-start.10 = (f32[64,16,128]{2,0,1:T(8,128)S(1)}, f32[64,16,128]{2,0,1:T(8,128)S(1)}, u32[]{:S(2)}, u32[]{:S(2)}) collective-permute-start(f32[64,16,128]{2,0,1:T(8,128)S(1)} %broadcast_select_fusion.2), channel_id=1, source_target_pairs={{0,2},{1,3},{2,4},{3,5},{4,6},{5,7},{6,8},{7,9},{8,10},{9,11},{10,... | collective-permute-start | bytes 1572872 | tf_op jit(solution)/shard_map/ppermute | solution.py:17
  135.0 28.3 %copy-start.4 = (f32[8,2,1,16384]{3,2,1,0:T(1,128)S(1)}, f32[8,2,1,16384]{3,2,1,0:T(1,128)}, u32[]{:S(2)}) copy-start(f32[8,2,1,16384]{3,2,1,0:T(1,128)} %param.11) | copy-start | bytes 3145732
  135.1 33.6 %collective-permute-start.4 = (f32[64,16,128]{2,0,1:T(8,128)S(1)}, f32[64,16,128]{2,0,1:T(8,128)S(1)}, u32[]{:S(2)}, u32[]{:S(2)}) collective-permute-start(f32[64,16,128]{2,0,1:T(8,128)S(1)} %broadcast_select_fusion.8), channel_id=1, source_target_pairs={{0,16},{1,17},{2,18},{3,19},{4,20},{5,21},{6,22},{7,23},{8,24},{9,... | collective-permute-start | bytes 1572872 | tf_op jit(solution)/shard_map/ppermute | solution.py:17
  137.2 40.9 %collective-permute-start.11 = (f32[64,16,128]{2,0,1:T(8,128)S(1)}, f32[64,16,128]{2,0,1:T(8,128)}, u32[]{:S(2)}, u32[]{:S(2)}) collective-permute-start(f32[64,16,128]{2,0,1:T(8,128)S(1)} %broadcast_select_fusion.3), channel_id=1, source_target_pairs={{0,1},{1,2},{2,3},{3,4},{4,5},{5,6},{6,7},{7,8},{8,9},{9,10},{10,1... | collective-permute-start | bytes 1572872 | tf_op jit(solution)/shard_map/ppermute | solution.py:17
  165.1 25.5 %all-to-all-start = ((f32[8,2,128,128]{3,1,0,2:T(2,128)}), f32[8,2,128,128]{3,1,0,2:T(2,128)S(1)}, u32[]{:S(2)}, u32[]{:S(2)}) async-start(f32[8,2,128,128]{3,1,0,2:T(2,128)} %copy.35), calls=%async_computation | async-start | bytes 2097152 | tf_op jit(solution)/shard_map/all_to_all | solution.py:61
  168.8 31.6 %collective-permute-start.5 = (f32[64,16,128]{2,0,1:T(8,128)S(1)}, f32[64,16,128]{2,0,1:T(8,128)S(1)}, u32[]{:S(2)}, u32[]{:S(2)}) collective-permute-start(f32[64,16,128]{2,0,1:T(8,128)S(1)} %broadcast_select_fusion.9), channel_id=1, source_target_pairs={{0,31},{1,0},{2,1},{3,2},{4,3},{5,4},{6,5},{7,6},{8,7},{9,8},{10,9... | collective-permute-start | bytes 1572872 | tf_op jit(solution)/shard_map/ppermute | solution.py:17
  170.7 29.8 %collective-permute-start.6 = (f32[64,16,128]{2,0,1:T(8,128)S(1)}, f32[64,16,128]{2,0,1:T(8,128)}, u32[]{:S(2)}, u32[]{:S(2)}) collective-permute-start(f32[64,16,128]{2,0,1:T(8,128)S(1)} %broadcast_select_fusion.9), channel_id=1, source_target_pairs={{0,1},{1,2},{2,3},{3,4},{4,5},{5,6},{6,7},{7,8},{8,9},{9,10},{10,1... | collective-permute-start | bytes 1572872 | tf_op jit(solution)/shard_map/ppermute | solution.py:17
  179.3 31.6 %collective-permute-start.12 = (f32[64,16,128]{2,0,1:T(8,128)S(1)}, f32[64,16,128]{2,0,1:T(8,128)S(1)}, u32[]{:S(2)}, u32[]{:S(2)}) collective-permute-start(f32[64,16,128]{2,0,1:T(8,128)S(1)} %broadcast_select_fusion.4), channel_id=1, source_target_pairs={{0,31},{1,0},{2,1},{3,2},{4,3},{5,4},{6,5},{7,6},{8,7},{9,8},{10,9... | collective-permute-start | bytes 1572872 | tf_op jit(solution)/shard_map/ppermute | solution.py:17
  185.6 25.3 %collective-permute-start.13 = (f32[64,16,128]{2,0,1:T(8,128)S(1)}, f32[64,16,128]{2,0,1:T(8,128)}, u32[]{:S(2)}, u32[]{:S(2)}) collective-permute-start(f32[64,16,128]{2,0,1:T(8,128)S(1)} %broadcast_select_fusion.4), channel_id=1, source_target_pairs={{0,1},{1,2},{2,3},{3,4},{4,5},{5,6},{6,7},{7,8},{8,9},{9,10},{10,1... | collective-permute-start | bytes 1572872 | tf_op jit(solution)/shard_map/ppermute | solution.py:17
  232.9 1.2 copy-start.3
